TPU v7x, 32 devices: a whole 2x2x4 slice. The times are simulated.
32 devices in a mesh: rep: 2 (over x), exp: 16 (over z, y, core).
Axes of the slice: x: 2, y: 2, z: 4, core: 2. Of those that a mesh axis runs over, the one named last changes fastest.
Arguments:
- tokens: bfloat16 [2, 2048, 2048], P('rep', 'exp'), may hold values from -6 to 6
- cotangent: bfloat16 [2, 2048, 2048], P('rep', 'exp'), may hold values from -6 to 6
- routes: int32 [2, 2048, 8], P('rep', 'exp'), may hold values from 0 to 15, all different within a row; in each aligned block of 128 rows (0 to 127, 128 to 255, ..., all dimensions but the last counted through in order) at most 96 rows name the same one
- router_pair_weight: bfloat16 [2, 2048, 8], P('rep', 'exp'), may hold values from 0.019897461 to 0.5
- capacity: int32 [16], replicated, may hold values from 512 to 1024, as said below
- training_step_index: int32 [1], replicated, may hold values from 0 to 999
- frozen_gate_matrix: bfloat16 [16, 2048, 768], P('exp'), may hold values from -0.125 to 0.125
- frozen_up_matrix: bfloat16 [16, 2048, 768], P('exp'), may hold values from -0.125 to 0.125
- frozen_down_matrix: bfloat16 [16, 768, 2048], P('exp'), may hold values from -0.21875 to 0.21875
- adapter_input_factor: float32 [2, 16, 16, 768], P('rep', 'exp'), may hold values from -0.6 to 0.6
- adapter_output_factor: float32 [2, 16, 16, 2048], P('rep', 'exp'), may hold values from -1.5 to 1.5
- input_first_moment: float32 [2, 16, 16, 768], P('rep', 'exp'), may hold values from -2 to 2
- output_first_moment: float32 [2, 16, 16, 2048], P('rep', 'exp'), may hold values from -2 to 2
- input_second_moment: float32 [2, 16, 16, 768], P('rep', 'exp'), may hold values from 0.05 to 5
- output_second_moment: float32 [2, 16, 16, 2048], P('rep', 'exp'), may hold values from 0.05 to 5
Outputs:
- combined: bfloat16 [2, 2048, 2048], P('rep', 'exp')
- new_lora_in: float32 [2, 16, 16, 768], P('rep', 'exp')
- new_lora_out: float32 [2, 16, 16, 2048], P('rep', 'exp')
- new_first_in: float32 [2, 16, 16, 768], P('rep', 'exp')
- new_first_out: float32 [2, 16, 16, 2048], P('rep', 'exp')
- new_second_in: float32 [2, 16, 16, 768], P('rep', 'exp')
- new_second_out: float32 [2, 16, 16, 2048], P('rep', 'exp')
Inputs may be any that keep to these rules, and one draw needn't show every extreme that they name: `routes`: in the rows of one device, no expert is named more than 96 times; a token names distinct experts. The largest capacity is exactly 1024.
All inputs are finite; a program needn't handle non-finite values.
Results may differ from a plain program's by a relative error of at most 0.007.
Values may be sent and summed in bfloat16 or wider, within the bound.
A program may use at most 128 MiB of HBM per device.

v0:
```python
from functools import partial

import jax
import jax.numpy as jnp
from jax import lax
from jax.sharding import PartitionSpec as P

adapter_scale = 0.5
beta_one = 0.9
beta_two = 0.999
learn_rate = 0.02
weight_decay = 0.01
epsilon = 1e-08


def as_sent(x):
    return jax.tree.map(lambda a: a.astype(jnp.bfloat16) if a.dtype == jnp.float32 else a, x)


def partner(value, axis, stride):
    mask = 2**stride
    pairs = [(source, source ^ mask) for source in range(lax.axis_size(axis))]
    return lax.ppermute(value, axis, pairs)


def swap_with(joined_rows, level_bit):
    return jax.tree.map(
        lambda part, own: part.astype(own.dtype),
        partner(as_sent(joined_rows), "rep", level_bit),
        joined_rows,
    )


def adam_update(averaged, gradient, first_moment, second_moment, fix_one, fix_two):
    new_first = beta_one * first_moment + (1.0 - beta_one) * gradient
    new_second = beta_two * second_moment + (1.0 - beta_two) * gradient * gradient
    stepped = new_first / fix_one / (jnp.sqrt(new_second / fix_two) + epsilon)
    return (averaged - learn_rate * (stepped + weight_decay * averaged), new_first, new_second)


def per_device(
    tokens,
    cotangent,
    routes,
    router_pair_weight,
    capacity,
    training_step_index,
    frozen_gate_matrix,
    frozen_up_matrix,
    frozen_down_matrix,
    adapter_input_factor,
    adapter_output_factor,
    input_first_moment,
    output_first_moment,
    input_second_moment,
    output_second_moment,
):
    devices = lax.axis_size("exp")
    me = lax.axis_index("exp")
    assert frozen_gate_matrix.shape[0] == 1
    tok_dev, width = tokens.shape[1:]
    rank = adapter_output_factor.shape[2]
    own_grads = cotangent[0]
    in_b = adapter_input_factor[0, 0].astype(jnp.bfloat16)
    out_b = adapter_output_factor[0, 0].astype(jnp.bfloat16)

    hits = routes[0][None, :, :] == jnp.arange(devices, dtype=jnp.int32)[:, None, None]
    table = jnp.sum(
        jnp.where(hits, router_pair_weight[0].astype(jnp.float32)[None], 0.0), axis=2
    ).astype(jnp.bfloat16)
    small = jnp.concatenate((out_b, table.reshape(-1, width)), axis=0)
    small_all = lax.all_gather(small, "exp")
    rows_all = lax.all_gather(tokens[0], "exp", tiled=True)

    out_all = small_all[:, :rank].reshape(devices * rank, width)
    table_all = small_all[:, rank:].reshape(devices, devices, tok_dev).astype(jnp.float32)
    hit_all = (table_all > 0).astype(jnp.float32)
    earlier = jnp.triu(jnp.ones((tok_dev, tok_dev), jnp.float32), 1)
    within = jnp.einsum("set,tu->seu", hit_all, earlier)
    counts = jnp.sum(hit_all, axis=2)
    start = jnp.cumsum(counts, axis=0) - counts
    position = start[:, :, None] + within
    kept = position < capacity.astype(jnp.float32)[None, :, None]
    table_all = jnp.where(kept, table_all, 0.0)
    own_table = lax.dynamic_index_in_dim(table_all, me, 0, keepdims=False)
    expert_weight = lax.dynamic_index_in_dim(table_all, me, 1, keepdims=False).reshape(-1)

    back = jnp.einsum("td,cd->tc", own_grads, out_all, preferred_element_type=jnp.float32)
    back = back.reshape(tok_dev, devices, rank).transpose(1, 0, 2) * own_table[:, :, None]
    back = lax.all_to_all(back.astype(jnp.bfloat16), "exp", 0, 0, tiled=True)
    back = back.reshape(devices * tok_dev, rank)

    gate = jnp.dot(rows_all, frozen_gate_matrix[0], preferred_element_type=jnp.float32)
    upper = jnp.dot(rows_all, frozen_up_matrix[0], preferred_element_type=jnp.float32)
    hidden = (jax.nn.silu(gate) * upper).astype(jnp.bfloat16)
    low = jnp.einsum("nf,rf->nr", hidden, in_b, preferred_element_type=jnp.float32).astype(
        jnp.bfloat16
    )
    low_back = lax.all_to_all(low.reshape(devices, tok_dev, rank), "exp", 0, 0, tiled=True)
    result = jnp.dot(
        hidden, frozen_down_matrix[0], preferred_element_type=jnp.float32
    ) + adapter_scale * jnp.dot(low, out_b, preferred_element_type=jnp.float32)
    result = (expert_weight[:, None] * result).astype(jnp.bfloat16)
    combined = lax.psum_scatter(result, "exp", scatter_dimension=0, tiled=True)[None]

    grad_in = adapter_scale * jnp.einsum(
        "nr,nf->rf", back, hidden, preferred_element_type=jnp.float32
    )
    weighted = (low_back.astype(jnp.float32) * own_table[:, :, None]).astype(jnp.bfloat16)
    grad_out = adapter_scale * jnp.einsum(
        "etr,td->erd", weighted, own_grads, preferred_element_type=jnp.float32
    )
    grad_out = lax.psum_scatter(
        grad_out.reshape(devices * rank, width), "exp", scatter_dimension=0, tiled=True
    )

    levels = lax.axis_size("rep").bit_length() - 1
    joined_rows = jnp.concatenate((adapter_input_factor[0], adapter_output_factor[0]), axis=2)
    branches = [partial(swap_with, level_bit=level_value) for level_value in range(levels)]
    gossip_neighbor = lax.switch(training_step_index[0] % levels, branches, joined_rows)
    units = adapter_input_factor.shape[3]
    mean_in = 0.5 * (adapter_input_factor[0] + gossip_neighbor[:, :, :units])
    mean_out = 0.5 * (adapter_output_factor[0] + gossip_neighbor[:, :, units:])
    power = (training_step_index[0] + 1).astype(jnp.float32)
    fix_one = 1.0 - jnp.power(jnp.float32(beta_one), power)
    fix_two = 1.0 - jnp.power(jnp.float32(beta_two), power)
    new_in, new_first_in, new_second_in = adam_update(
        mean_in, grad_in[None], input_first_moment[0], input_second_moment[0], fix_one, fix_two
    )
    new_out, new_first_out, new_second_out = adam_update(
        mean_out, grad_out[None], output_first_moment[0], output_second_moment[0], fix_one, fix_two
    )
    return (
        combined,
        new_in[None],
        new_out[None],
        new_first_in[None],
        new_first_out[None],
        new_second_in[None],
        new_second_out[None],
    )


def solution(mesh):
    placed = (
        P("rep", "exp", None),
        P("rep", "exp", None),
        P("rep", "exp", None),
        P("rep", "exp", None),
        P(),
        P(),
        P("exp", None, None),
        P("exp", None, None),
        P("exp", None, None),
        P("rep", "exp", None, None),
        P("rep", "exp", None, None),
        P("rep", "exp", None, None),
        P("rep", "exp", None, None),
        P("rep", "exp", None, None),
        P("rep", "exp", None, None),
    )
    return jax.shard_map(
        per_device,
        mesh=mesh,
        in_specs=placed,
        out_specs=(
            P("rep", "exp", None),
            P("rep", "exp", None, None),
            P("rep", "exp", None, None),
            P("rep", "exp", None, None),
            P("rep", "exp", None, None),
            P("rep", "exp", None, None),
            P("rep", "exp", None, None),
        ),
        check_vma=False,
    )
```

profile of v0, /device:TPU:0, one launch (start us, length us, event | category | flops | bytes accessed | tf_op | source)
XLA Modules:
  0.0 338.8 jit_solution(9093886024028535779)
XLA Ops:
  7.2 1.8 bitcast_convert_fusion
  12.5 41.1 %all-gather.8.cloned.1.call-done = bf16[16,17,2048]{2,1,0:T(8,128)(2,1)} async-done(((bf16[1,17,2048]{2,1,0:T(8,128)(2,1)}), bf16[16,17,2048]{2,1,0:T(8,128)(2,1)}) %all-gather.8.cloned.1.call-update) | async-done | bytes 1114128 | tf_op jit(solution)/shard_map/all_gather | solution.py:72
  54.9 74.7 %all-gather.6.cloned.1.call-done = bf16[1,2048,2048]{2,1,0:T(8,128)(2,1)} async-done(((bf16[1,128,2048]{2,1,0:T(8,128)(2,1)}), bf16[1,2048,2048]{2,1,0:T(8,128)(2,1)}) %all-gather.6.cloned.1.call-update) | async-done | bytes 8388624 | tf_op jit(solution)/shard_map/all_gather | solution.py:73
  129.6 10.1 %fusion.2 = f32[2048,768]{1,0:T(8,128)S(1)} fusion(bf16[1,2048,2048]{2,1,0:T(8,128)(2,1)} %all-gather.6.cloned.1.call-done, bf16[1,2048,768]{2,1,0:T(8,128)(2,1)} %param.21), kind=kOutput, calls=%fused_computation.3 | convolution fusion | flops 6442450944 | bytes 17825792 | tf_op jit(solution)/shard_map/dot_general | solution.py:93
  139.8 7.4 %multiply_convert_fusion.1 = bf16[2048,768]{1,0:T(8,128)(2,1)S(1)} fusion(f32[2048,768]{1,0:T(8,128)S(1)} %fusion.2, bf16[1,2048,2048]{2,1,0:T(8,128)(2,1)S(1)} %copy-done.7, bf16[1,2048,768]{2,1,0:T(8,128)(2,1)S(1)} %copy-done.8), kind=kOutput, calls=%fused_computation.5 | convolution fusion | flops 6451888128 | bytes 20971520 | tf_op jit(solution)/shard_map/dot_general | solution.py:94
  147.2 1.7 copy-done.1
  150.5 4.2 %all-to-all-start.1 = ((bf16[16,128,16]{1,2,0:T(8,128)(2,1)}), bf16[16,128,16]{1,2,0:T(8,128)(2,1)}, u32[]{:S(2)}, u32[]{:S(2)}) async-start(bf16[16,128,16]{1,2,0:T(8,128)(2,1)} %copy_bitcast_fusion), calls=%async_computation.2 | async-start | bytes 131072 | tf_op jit(solution)/shard_map/all_to_all | solution.py:99
  155.5 6.0 %all-to-all-done.1 = bf16[16,128,16]{1,2,0:T(8,128)(2,1)} async-done(((bf16[16,128,16]{1,2,0:T(8,128)(2,1)}), bf16[16,128,16]{1,2,0:T(8,128)(2,1)}, u32[]{:S(2)}, u32[]{:S(2)}) %all-to-all-start.1) | async-done | bytes 65568 | tf_op jit(solution)/shard_map/all_to_all | solution.py:99
  161.5 3.0 convolution_multiply_fusion
  165.4 12.1 %fusion.6 = f32[2048,2048]{1,0:T(8,128)} fusion(bf16[2048,768]{1,0:T(8,128)(2,1)} %copy-done.1, bf16[1,768,2048]{2,1,0:T(8,128)(2,1)S(1)} %copy-done), kind=kOutput, calls=%fused_computation.6 | convolution fusion | flops 6442450944 | bytes 23068672 | tf_op jit(solution)/shard_map/dot_general | solution.py:100
  177.5 9.6 %multiply_convert_fusion = bf16[2048,2048]{1,0:T(8,128)(2,1)} fusion(f32[2048,2048]{1,0:T(8,128)} %fusion.6, bf16[2048,16]{0,1:T(8,128)(2,1)S(1)} %convolution_convert_fusion, bf16[16,2048]{1,0:T(8,128)(2,1)S(1)} %get-tuple-element.10, f32[2048]{0:T(1024)S(1)} %bitcast.142), kind=kOutput, calls=%fused_computation | convolution fusion | flops 150994944 | bytes 25305088 | tf_op jit(solution)/shard_map/dot_general | solution.py:102
  187.2 1.4 slice.18
  188.5 1.5 fusion.13
  190.7 4.2 %all-to-all-start = ((bf16[16,128,16]{1,2,0:T(8,128)(2,1)}), bf16[16,128,16]{1,2,0:T(8,128)(2,1)}, u32[]{:S(2)}, u32[]{:S(2)}) async-start(bf16[16,128,16]{1,2,0:T(8,128)(2,1)} %multiply_convert_fusion.3), calls=%async_computation.1 | async-start | bytes 131072 | tf_op jit(solution)/shard_map/all_to_all | solution.py:90
  194.9 1.6 collective-permute-start
  197.2 2.5 collective-permute-done
  199.7 2.8 all-to-all-done
  202.5 2.5 fusion.19
  204.9 1.5 fusion.35
  206.4 1.5 fusion.27
  207.9 15.7 %reduce-scatter.5.cloned.1.call-done = f32[16,2048]{1,0:T(8,128)} async-done(((f32[256,2048]{1,0:T(8,128)}), f32[16,2048]{1,0:T(8,128)}) %reduce-scatter.5.cloned.1.call-update) | async-done | bytes 131088 | tf_op jit(solution)/shard_map/reduce_scatter | solution.py:113
  223.6 1.7 fusion.29
  225.3 1.8 fusion.18
  227.1 105.2 %reduce-scatter.3.cloned.1.call-done = bf16[128,2048]{1,0:T(8,128)(2,1)} async-done(((bf16[2048,2048]{1,0:T(8,128)(2,1)}), bf16[128,2048]{1,0:T(8,128)(2,1)}) %reduce-scatter.3.cloned.1.call-update) | async-done | bytes 524304 | tf_op jit(solution)/shard_map/reduce_scatter | solution.py:104
  (43 shorter events, 8.8 us)
Async XLA Ops:
  7.2 158.3 %copy-start = (bf16[1,768,2048]{2,1,0:T(8,128)(2,1)S(1)}, bf16[1,768,2048]{2,1,0:T(8,128)(2,1)}, u32[]{:S(2)}) copy-start(bf16[1,768,2048]{2,1,0:T(8,128)(2,1)} %param.23) | copy-start | bytes 9437188
  7.2 46.4 %all-gather.8.cloned.1.call-start = ((), (), s32[]{:S(2)}) async-start(), calls=%async_computation.7 | async-start | bytes 1671168 | tf_op jit(solution)/shard_map/all_gather | solution.py:72
  11.1 118.5 %all-gather.6.cloned.1.call-start = ((), (), s32[]{:S(2)}) async-start(), calls=%async_computation.6 | async-start | bytes 8912896 | tf_op jit(solution)/shard_map/all_gather | solution.py:73
  129.6 10.2 %copy-start.7 = (bf16[1,2048,2048]{2,1,0:T(8,128)(2,1)S(1)}, bf16[1,2048,2048]{2,1,0:T(8,128)(2,1)}, u32[]{:S(2)}) copy-start(bf16[1,2048,2048]{2,1,0:T(8,128)(2,1)} %all-gather.6.cloned.1.call-done) | copy-start | bytes 25165828
  129.6 10.2 %copy-start.8 = (bf16[1,2048,768]{2,1,0:T(8,128)(2,1)S(1)}, bf16[1,2048,768]{2,1,0:T(8,128)(2,1)}, u32[]{:S(2)}) copy-start(bf16[1,2048,768]{2,1,0:T(8,128)(2,1)} %param.22) | copy-start | bytes 9437188
  139.8 9.1 %copy-start.3 = (f32[1,1,16,768]{3,2,1,0:T(8,128)S(1)}, f32[1,1,16,768]{3,2,1,0:T(8,128)}, u32[]{:S(2)}) copy-start(f32[1,1,16,768]{3,2,1,0:T(8,128)} %param.24) | copy-start | bytes 147460
  147.2 1.7 copy-start.1
  150.5 11.1 %all-to-all-start.1 = ((bf16[16,128,16]{1,2,0:T(8,128)(2,1)}), bf16[16,128,16]{1,2,0:T(8,128)(2,1)}, u32[]{:S(2)}, u32[]{:S(2)}) async-start(bf16[16,128,16]{1,2,0:T(8,128)(2,1)} %copy_bitcast_fusion), calls=%async_computation.2 | async-start | bytes 131072 | tf_op jit(solution)/shard_map/all_to_all | solution.py:99
  154.6 69.0 %reduce-scatter.5.cloned.1.call-start = ((), (), s32[]{:S(2)}) async-start(), calls=%async_computation.5 | async-start | bytes 2228224 | tf_op jit(solution)/shard_map/reduce_scatter | solution.py:113
  154.8 0.7 copy-start.6
  164.5 167.8 %reduce-scatter.3.cloned.1.call-start = ((), (), s32[]{:S(2)}) async-start(), calls=%async_computation.4 | async-start | bytes 8912896 | tf_op jit(solution)/shard_map/reduce_scatter | solution.py:104
  187.1 7.7 %copy-start.4 = (bf16[1,16,2048]{2,1,0:T(8,128)(2,1)S(1)}, bf16[1,16,2048]{2,1,0:T(8,128)(2,1)}, u32[]{:S(2)}) copy-start(bf16[1,16,2048]{2,1,0:T(8,128)(2,1)} %get-tuple-element.9) | copy-start | bytes 196612
  187.1 17.8 %copy-start.5 = (f32[1,1,16,768]{3,2,1,0:T(8,128)S(1)}, f32[1,1,16,768]{3,2,1,0:T(8,128)}, u32[]{:S(2)}) copy-start(f32[1,1,16,768]{3,2,1,0:T(8,128)} %param.26) | copy-start | bytes 147460
  187.1 36.5 %copy-start.2 = (f32[1,1,16,2048]{3,2,1,0:T(8,128)S(1)}, f32[1,1,16,2048]{3,2,1,0:T(8,128)}, u32[]{:S(2)}) copy-start(f32[1,1,16,2048]{3,2,1,0:T(8,128)} %param.27) | copy-start | bytes 393220
  190.7 11.8 %all-to-all-start = ((bf16[16,128,16]{1,2,0:T(8,128)(2,1)}), bf16[16,128,16]{1,2,0:T(8,128)(2,1)}, u32[]{:S(2)}, u32[]{:S(2)}) async-start(bf16[16,128,16]{1,2,0:T(8,128)(2,1)} %multiply_convert_fusion.3), calls=%async_computation.1 | async-start | bytes 131072 | tf_op jit(solution)/shard_map/all_to_all | solution.py:90
  194.9 4.8 %collective-permute-start = (bf16[1,16,2816]{2,1,0:T(8,128)(2,1)S(1)}, bf16[1,16,2816]{2,1,0:T(8,128)(2,1)S(1)}, u32[]{:S(2)}, u32[]{:S(2)}) collective-permute-start(bf16[1,16,2816]{2,1,0:T(8,128)(2,1)S(1)} %pad_maximum_fusion), channel_id=1, source_target_pairs={{0,16},{16,0},{1,17},{17,1},{2,18},{18,2},{3,19},{19,3},{4,20},{20... | collective-permute-start | bytes 270344 | tf_op jit(solution)/shard_map/ppermute | solution.py:23
Sparse Core Ops, SparseCore 0:
  11.2 42.3 all-gather.7
  55.8 73.7 all-gather.5
  164.6 58.9 reduce-scatter.4
  228.6 103.5 reduce-scatter.2
where the time goes:
time: 340 us; the launch traced here: 339 us
  waiting for transfers between devices  249 us (73%)
  matrix products  47.2 us (14%)
  between operations  14.7 us (4%)
  other arithmetic  12.9 us (4%)
  starting transfers between devices  10.1 us (3%)
  local copies, waits for them, and re-layouts  5.29 us (2%)
    reduce_scatter x1, waiting for transfers between devices, per_device(): lax.psum_scatter(result, 'exp', scatter_dimension=0, tiled=True)[None]  105 us
    all_gather x1, waiting for transfers between devices, per_device(): rows_all = lax.all_gather(tokens[0], 'exp', tiled=True)  74.7 us
    all_gather x1, waiting for transfers between devices, per_device(): small_all = lax.all_gather(small, 'exp')  41.1 us
    reduce_scatter x1, waiting for transfers between devices, per_device(): lax.psum_scatter(grad_out.reshape(devices * rank, width), 'exp', scatter_...  15.7 us
    dot_general x1, matrix products, per_device(): jnp.dot(hidden, frozen_down_matrix[0], preferred_element_type=jnp.float32)  12.1 us
    dot_general x1, matrix products, per_device(): jnp.dot(rows_all, frozen_gate_matrix[0], preferred_element_type=jnp.float32)  10.1 us
    dot_general x1, matrix products, per_device(): jnp.dot(low, out_b, preferred_element_type=jnp.float32)  9.57 us
    dot_general x1, matrix products, per_device(): jnp.dot(rows_all, frozen_up_matrix[0], preferred_element_type=jnp.float32)  7.39 us
  transfers between devices with their start and end apart: 7, of which 7 were waited for; matrix products, arithmetic and copies ran while one was open for 11% of the time, Pallas kernels for 0%

commit v1 on v0

v1 whole, which is shorter than its diff:
```python
from functools import partial

import jax
import jax.numpy as jnp
from jax import lax
from jax.experimental import pallas as pl
from jax.experimental.pallas import tpu as pltpu
from jax.sharding import PartitionSpec as P

adapter_scale = 0.5
beta_one = 0.9
beta_two = 0.999
learn_rate = 0.02
weight_decay = 0.01
epsilon = 1e-08
MESH = pl.DeviceIdType.MESH


def as_sent(x):
    return jax.tree.map(lambda a: a.astype(jnp.bfloat16) if a.dtype == jnp.float32 else a, x)


def partner(value, axis, stride):
    mask = 2**stride
    pairs = [(source, source ^ mask) for source in range(lax.axis_size(axis))]
    return lax.ppermute(value, axis, pairs)


def swap_with(joined_rows, level_bit):
    return jax.tree.map(
        lambda part, own: part.astype(own.dtype),
        partner(as_sent(joined_rows), "rep", level_bit),
        joined_rows,
    )


def adam_update(averaged, gradient, first_moment, second_moment, fix_one, fix_two):
    new_first = beta_one * first_moment + (1.0 - beta_one) * gradient
    new_second = beta_two * second_moment + (1.0 - beta_two) * gradient * gradient
    stepped = new_first / fix_one / (jnp.sqrt(new_second / fix_two) + epsilon)
    return (averaged - learn_rate * (stepped + weight_decay * averaged), new_first, new_second)


def layer_kernel(
    x_ref,
    cot_ref,
    table_ref,
    cap_ref,
    gate_ref,
    up_ref,
    down_ref,
    in_ref,
    out_ref,
    comb_ref,
    gin_ref,
    gout_ref,
    rows,
    part,
    from_core,
    from_y,
    from_low,
    from_high,
    hid,
    tables,
    low_mine,
    low_got,
    back_mine,
    back_got,
    grad_mine,
    grad_got,
    rows_s,
    rows_r,
    core_s,
    core_r,
    y_s,
    y_r,
    z_s,
    zu_r,
    zd_r,
    tab_s,
    tab_r,
    low_s,
    low_r,
    back_s,
    back_r,
    grad_s,
    grad_r,
):
    n = 16
    depth = 4
    f32 = jnp.float32
    bf16 = jnp.bfloat16
    me = lax.axis_index("exp")
    z, y, c = me // 4, (me // 2) % 2, me % 2
    tok = cot_ref.shape[0]
    rank = in_ref.shape[0]
    core_mate = me + 1 - 2 * c
    y_mate = me + 2 - 4 * y

    def copy(src, dst, send, recv, device):
        return pltpu.make_async_remote_copy(
            src_ref=src,
            dst_ref=dst,
            send_sem=send,
            recv_sem=recv,
            device_id={"exp": device},
            device_id_type=MESH,
        )

    def order(s):
        table = ((0, 1, 2, 3), (1, 2, 0, 3), (2, 1, 3, 0), (3, 2, 1, 0))
        value = s * 0
        for row in range(depth):
            for col in range(depth):
                value = jnp.where((z == row) & (s == col), table[row][col], value)
        return value

    def send_rows(kind, slot, device):
        return copy(rows.at[slot], rows.at[slot], rows_s.at[kind, slot], rows_r.at[slot], device)

    def send_table(d):
        return copy(
            table_ref, tables.at[me], tab_s.at[d], tab_r.at[me], lax.rem(me + d, n)
        )

    def send_low(t):
        return copy(low_mine.at[t], low_got.at[me], low_s.at[t], low_r.at[me], t)

    def send_back(t):
        return copy(back_mine.at[t], back_got.at[me], back_s.at[t], back_r.at[me], t)

    def send_grad(t):
        return copy(grad_mine.at[t], grad_got.at[me], grad_s.at[t], grad_r.at[me], t)

    def send_core(zt, yt):
        return copy(
            part.at[zt * 4 + yt * 2 + 1 - c],
            from_core.at[zt * 2 + yt],
            core_s.at[zt * 2 + yt],
            core_r.at[zt * 2 + yt],
            core_mate,
        )

    def send_y(zt):
        return copy(
            part.at[zt * 4 + (1 - y) * 2 + c], from_y.at[zt], y_s.at[zt], y_r.at[zt], y_mate
        )

    def send_up(zt):
        return copy(
            part.at[zt * 4 + y * 2 + c], from_low.at[zt], z_s.at[zt], zu_r.at[zt], me + 4
        )

    def send_down(zt):
        return copy(
            part.at[zt * 4 + y * 2 + c], from_high.at[zt], z_s.at[zt], zd_r.at[zt], me - 4
        )

    rows[me] = x_ref[...]
    tables[me] = table_ref[...]
    barrier = pltpu.get_barrier_semaphore()

    @pl.loop(1, n)
    def _(d):
        pl.semaphore_signal(
            barrier, inc=1, device_id={"exp": lax.rem(me + d, n)}, device_id_type=MESH
        )

    pl.semaphore_wait(barrier, n - 1)

    @pl.loop(1, n)
    def _(d):
        send_table(d).start()

    def forward(zz, act):
        slot = zz * 4 + y * 2 + c

        @pl.when((zz <= z) & (z < depth - 1))
        def _():
            act(send_rows(0, slot, me + 4))

        @pl.when((zz >= z) & (z > 0))
        def _():
            act(send_rows(1, slot, me - 4))

        act(send_rows(2, slot, y_mate))
        act(send_rows(3, slot, core_mate))

    forward(z, lambda one: one.start())

    @pl.loop(1, n)
    def _(d):
        source = lax.rem(me + d, n)
        copy(table_ref, tables.at[source], tab_s.at[d], tab_r.at[source], source).wait_recv()

    later = lax.broadcasted_iota(jnp.int32, (tok, tok), 1)
    sooner = lax.broadcasted_iota(jnp.int32, (tok, tok), 0)
    strictly = (sooner < later).astype(bf16)
    before = jnp.zeros((n, 1), f32)
    for source in range(n):
        weight = tables[source]
        hit = (weight > 0).astype(f32)
        within = jnp.dot(hit.astype(bf16), strictly, preferred_element_type=f32)
        kept = before + within < cap_ref[...]
        tables[source] = jnp.where(kept, weight, 0.0)
        before = before + jnp.sum(hit, axis=1, keepdims=True)

    own_table = tables.at[me]
    lane = lax.broadcasted_iota(jnp.int32, (tok, n), 1)

    def transposed_dot(a, b):
        return lax.dot_general(a, b, (((1,), (1,)), ((), ())), preferred_element_type=f32)

    def expert_pair(zt, yt):
        first = zt * 4 + yt * 2
        x = jnp.concatenate((rows[first, 0:tok, :], rows[first + 1, 0:tok, :]), axis=0)
        gate = jnp.dot(x, gate_ref[...], preferred_element_type=f32)
        upper = jnp.dot(x, up_ref[...], preferred_element_type=f32)
        hidden = (gate / (1.0 + jnp.exp(-gate)) * upper).astype(bf16)
        hid[first] = hidden[:tok]
        hid[first + 1] = hidden[tok:]
        low_t = transposed_dot(in_ref[...], hidden).astype(bf16)
        low = transposed_dot(hidden, in_ref[...]).astype(bf16)
        result = jnp.dot(hidden, down_ref[...], preferred_element_type=f32)
        result = result + adapter_scale * jnp.dot(low, out_ref[...], preferred_element_type=f32)
        for k in range(2):
            t = first + k
            scale = jnp.sum(
                jnp.where(lane == me, tables[t].T, 0.0), axis=1, keepdims=True
            )
            part[t] = (scale * result[k * tok : (k + 1) * tok]).astype(bf16)
            back = transposed_dot(rows[t, tok : tok + rank, :], cot_ref[...])
            back = (back * own_table[pl.ds(t, 1), :]).astype(bf16)
            low_k = low_t[:, k * tok : (k + 1) * tok]

            @pl.when(t == me)
            def _():
                low_got[t] = low_k
                back_got[t] = back

            @pl.when(t != me)
            def _():
                low_mine[t] = low_k
                back_mine[t] = back
                send_low(t).start()
                send_back(t).start()

        send_core(zt, yt).start()

    def wait_rows(slot):
        send_rows(3, slot, core_mate).wait_recv()

    def add_core(zt, yt):
        send_core(zt, yt).wait_recv()
        t = zt * 4 + yt * 2 + c
        part[t] = (part[t].astype(f32) + from_core[zt * 2 + yt].astype(f32)).astype(bf16)

    @pl.loop(0, depth + 2)
    def _(s):
        now = order(s)
        last = order(s - 1)
        older = order(s - 2)

        @pl.when((s > 0) & (s < depth))
        def _():
            wait_rows(now * 4 + y * 2 + c)
            forward(now, lambda one: one.start())

        @pl.when((s > 0) & (s <= depth))
        def _():
            slot = last * 4 + (1 - y) * 2 + c
            wait_rows(slot)
            send_rows(3, slot, core_mate).start()

        @pl.loop(0, 2)
        def _(which):
            zt = jnp.where(which == 0, now, last)
            yt = jnp.where(which == 0, y, 1 - y)

            @pl.when((s >= which) & (s < depth + which))
            def _():
                wait_rows(zt * 4 + yt * 2 + 1 - c)
                expert_pair(zt, yt)

        @pl.when(s >= 2)
        def _():
            t = older * 4 + y * 2 + c
            send_y(older).wait_recv()
            part[t] = (part[t].astype(f32) + from_y[older].astype(f32)).astype(bf16)

            @pl.when((z == 0) & (older > 0))
            def _():
                send_up(older).start()

            @pl.when((z == depth - 1) & (older < depth - 1))
            def _():
                send_down(older).start()

        @pl.when((s > 0) & (s <= depth))
        def _():
            add_core(last, 1 - y)
            send_y(last).start()

        @pl.when(s < depth)
        def _():
            add_core(now, y)

    @pl.when((z > 0) & (z < depth - 1))
    def _():
        @pl.loop(0, depth - 1)
        def _(item):
            up_first = jnp.where(item == 0, 2, jnp.where(item == 1, 3, 0))
            zt = jnp.where(z == 1, up_first, 3 - up_first)
            t = zt * 4 + y * 2 + c

            @pl.when(zt > z)
            def _():
                send_up(zt).wait_recv()
                part[t] = (part[t].astype(f32) + from_low[zt].astype(f32)).astype(bf16)
                send_up(zt).start()

            @pl.when(zt < z)
            def _():
                send_down(zt).wait_recv()
                part[t] = (part[t].astype(f32) + from_high[zt].astype(f32)).astype(bf16)
                send_down(zt).start()

    @pl.loop(0, n)
    def _(t):
        @pl.when(t != me)
        def _():
            copy(low_mine.at[t], low_got.at[t], low_s.at[t], low_r.at[t], t).wait_recv()

        weighted = (low_got[t].astype(f32) * own_table[pl.ds(t, 1), :]).astype(bf16)
        grad = adapter_scale * jnp.dot(weighted, cot_ref[...], preferred_element_type=f32)

        @pl.when(t == me)
        def _():
            grad_got[t] = grad.astype(bf16)

        @pl.when(t != me)
        def _():
            grad_mine[t] = grad.astype(bf16)
            send_grad(t).start()

    gin_ref[...] = jnp.zeros_like(gin_ref)

    @pl.loop(0, n)
    def _(t):
        @pl.when(t != me)
        def _():
            copy(back_mine.at[t], back_got.at[t], back_s.at[t], back_r.at[t], t).wait_recv()

        gin_ref[...] += adapter_scale * jnp.dot(
            back_got[t], hid[t], preferred_element_type=f32
        )

    gout_ref[...] = jnp.zeros_like(gout_ref)

    @pl.loop(0, n)
    def _(t):
        @pl.when(t != me)
        def _():
            copy(grad_mine.at[t], grad_got.at[t], grad_s.at[t], grad_r.at[t], t).wait_recv()

        gout_ref[...] += grad_got[t].astype(f32)

    @pl.when(z > 0)
    def _():
        send_up(z).wait_recv()

    @pl.when(z < depth - 1)
    def _():
        send_down(z).wait_recv()

    @pl.when(z == 0)
    def _():
        comb_ref[...] = (part[me].astype(f32) + from_high[z].astype(f32)).astype(bf16)

    @pl.when(z == depth - 1)
    def _():
        comb_ref[...] = (part[me].astype(f32) + from_low[z].astype(f32)).astype(bf16)

    @pl.when((z > 0) & (z < depth - 1))
    def _():
        comb_ref[...] = (
            part[me].astype(f32) + from_low[z].astype(f32) + from_high[z].astype(f32)
        ).astype(bf16)

    @pl.loop(0, depth)
    def _(zt):
        forward(zt, lambda one: one.wait_send())
        send_rows(3, zt * 4 + (1 - y) * 2 + c, core_mate).wait_send()
        send_core(zt, 0).wait_send()
        send_core(zt, 1).wait_send()
        send_y(zt).wait_send()

        @pl.when(zt != z)
        def _():
            copy(part.at[zt], from_low.at[zt], z_s.at[zt], zu_r.at[zt], y_mate).wait_send()

    @pl.loop(1, n)
    def _(d):
        t = lax.rem(me + d, n)
        send_table(d).wait_send()
        send_low(t).wait_send()
        send_back(t).wait_send()
        send_grad(t).wait_send()


def layer(x, cot, table, cap, gate, up, down, in_b, out_b):
    n = table.shape[0]
    tok, width = cot.shape
    rank, units = in_b.shape
    vmem = pl.BlockSpec(memory_space=pltpu.VMEM)
    bf16 = jnp.bfloat16
    dma = pltpu.SemaphoreType.DMA
    return pl.pallas_call(
        layer_kernel,
        out_shape=(
            jax.ShapeDtypeStruct((tok, width), bf16),
            jax.ShapeDtypeStruct((rank, units), jnp.float32),
            jax.ShapeDtypeStruct((rank, width), jnp.float32),
        ),
        in_specs=[vmem] * 9,
        out_specs=(vmem, vmem, vmem),
        scratch_shapes=[
            pltpu.VMEM((n, tok + rank, width), bf16),
            pltpu.VMEM((n, tok, width), bf16),
            pltpu.VMEM((n // 2, tok, width), bf16),
            pltpu.VMEM((n // 4, tok, width), bf16),
            pltpu.VMEM((n // 4, tok, width), bf16),
            pltpu.VMEM((n // 4, tok, width), bf16),
            pltpu.VMEM((n, tok, units), bf16),
            pltpu.VMEM((n, n, tok), jnp.float32),
            pltpu.VMEM((n, rank, tok), bf16),
            pltpu.VMEM((n, rank, tok), bf16),
            pltpu.VMEM((n, rank, tok), bf16),
            pltpu.VMEM((n, rank, tok), bf16),
            pltpu.VMEM((n, rank, width), bf16),
            pltpu.VMEM((n, rank, width), bf16),
            dma((4, n)),
            dma((n,)),
            dma((n // 2,)),
            dma((n // 2,)),
            dma((n // 4,)),
            dma((n // 4,)),
            dma((n // 4,)),
            dma((n // 4,)),
            dma((n // 4,)),
        ]
        + [dma((n,))] * 8,
        compiler_params=pltpu.CompilerParams(
            collective_id=0, has_side_effects=True, vmem_limit_bytes=60 * 1024 * 1024
        ),
        cost_estimate=pl.CostEstimate(
            flops=20_000_000_000, bytes_accessed=30_000_000, transcendentals=0
        ),
    )(x, cot, table, cap, gate, up, down, in_b, out_b)


def per_device(
    tokens,
    cotangent,
    routes,
    router_pair_weight,
    capacity,
    training_step_index,
    frozen_gate_matrix,
    frozen_up_matrix,
    frozen_down_matrix,
    adapter_input_factor,
    adapter_output_factor,
    input_first_moment,
    output_first_moment,
    input_second_moment,
    output_second_moment,
):
    devices = lax.axis_size("exp")
    assert frozen_gate_matrix.shape[0] == 1 and devices == 16
    own_grads = cotangent[0]
    in_b = adapter_input_factor[0, 0].astype(jnp.bfloat16)
    out_b = adapter_output_factor[0, 0].astype(jnp.bfloat16)

    hits = routes[0][None, :, :] == jnp.arange(devices, dtype=jnp.int32)[:, None, None]
    table = jnp.sum(
        jnp.where(hits, router_pair_weight[0].astype(jnp.float32)[None], 0.0), axis=2
    )
    combined, grad_in, grad_out = layer(
        jnp.concatenate((tokens[0], out_b), axis=0),
        own_grads,
        table,
        capacity.astype(jnp.float32)[:, None],
        frozen_gate_matrix[0],
        frozen_up_matrix[0],
        frozen_down_matrix[0],
        in_b,
        out_b,
    )
    combined = combined[None]

    levels = lax.axis_size("rep").bit_length() - 1
    joined_rows = jnp.concatenate((adapter_input_factor[0], adapter_output_factor[0]), axis=2)
    branches = [partial(swap_with, level_bit=level_value) for level_value in range(levels)]
    gossip_neighbor = lax.switch(training_step_index[0] % levels, branches, joined_rows)
    units = adapter_input_factor.shape[3]
    mean_in = 0.5 * (adapter_input_factor[0] + gossip_neighbor[:, :, :units])
    mean_out = 0.5 * (adapter_output_factor[0] + gossip_neighbor[:, :, units:])
    power = (training_step_index[0] + 1).astype(jnp.float32)
    fix_one = 1.0 - jnp.power(jnp.float32(beta_one), power)
    fix_two = 1.0 - jnp.power(jnp.float32(beta_two), power)
    new_in, new_first_in, new_second_in = adam_update(
        mean_in, grad_in[None], input_first_moment[0], input_second_moment[0], fix_one, fix_two
    )
    new_out, new_first_out, new_second_out = adam_update(
        mean_out, grad_out[None], output_first_moment[0], output_second_moment[0], fix_one, fix_two
    )
    return (
        combined,
        new_in[None],
        new_out[None],
        new_first_in[None],
        new_first_out[None],
        new_second_in[None],
        new_second_out[None],
    )


def solution(mesh):
    placed = (
        P("rep", "exp", None),
        P("rep", "exp", None),
        P("rep", "exp", None),
        P("rep", "exp", None),
        P(),
        P(),
        P("exp", None, None),
        P("exp", None, None),
        P("exp", None, None),
        P("rep", "exp", None, None),
        P("rep", "exp", None, None),
        P("rep", "exp", None, None),
        P("rep", "exp", None, None),
        P("rep", "exp", None, None),
        P("rep", "exp", None, None),
    )
    return jax.shard_map(
        per_device,
        mesh=mesh,
        in_specs=placed,
        out_specs=(
            P("rep", "exp", None),
            P("rep", "exp", None, None),
            P("rep", "exp", None, None),
            P("rep", "exp", None, None),
            P("rep", "exp", None, None),
            P("rep", "exp", None, None),
            P("rep", "exp", None, None),
        ),
        check_vma=False,
    )
```

time: 340 us -> 192 us (0.56)
  waiting for transfers between devices: 249 us -> 0.01 us
  Pallas kernels: 0 us -> 170 us
  matrix products: 47.2 us -> 0 us
  between operations: 14.7 us -> 1.46 us
  starting transfers between devices: 10.1 us -> 3 us
    pallas_call x0 -> x1, Pallas kernels: none -> 170 us  [layer(): pl.pallas_call(layer_kernel, out_shape=(jax.ShapeDtypeStruct((tok, width)...]
    reduce_scatter x2 -> x0, waiting for transfers between devices: 121 us -> none  [the longest x1 105 us: per_device(): lax.psum_scatter(result, 'exp', scatter_dimension=0, tiled=True)[None]]
    all_gather x2 -> x0, waiting for transfers between devices: 116 us -> none  [the longest x1 74.7 us: per_device(): rows_all = lax.all_gather(tokens[0], 'exp', tiled=True)]
    dot_general x9 -> x0, matrix products: 47.2 us -> none  [the longest x1 12.1 us: per_device(): jnp.dot(hidden, frozen_down_matrix[0], preferred_element_type=jnp.float32)]
    all_to_all x2 -> x0, waiting for transfers between devices: 8.79 us -> none  [the longest x1 6.03 us: per_device(): lax.all_to_all(low.reshape(devices, tok_dev, rank), 'exp', 0, 0, tiled=True)]
    all_to_all x2 -> x0, starting transfers between devices: 8.31 us -> none  [the longest x1 4.16 us: per_device(): back = lax.all_to_all(back.astype(jnp.bfloat16), 'exp', 0, 0, tiled=True)]
  transfers between devices with their start and end apart: 7 -> 1, of which waited for: 7 -> 0; matrix products, arithmetic and copies ran while one was open for 11% -> 4% of each run, Pallas kernels for 0% -> 89%
where the time goes in v1:
time: 192 us; the launch traced here: 190 us
  Pallas kernels  170 us (89%)
  other arithmetic  13.3 us (7%)
  starting transfers between devices  3 us (2%)
  local copies, waits for them, and re-layouts  2.6 us (1%)
    pallas_call x1, Pallas kernels, layer(): pl.pallas_call(layer_kernel, out_shape=(jax.ShapeDtypeStruct((tok, width)...  170 us
  transfers between devices with their start and end apart: 1, of which 0 were waited for; matrix products, arithmetic and copies ran while one was open for 4% of the time, Pallas kernels for 89%

profile of v1, /device:TPU:0, one launch (start us, length us, event | category | flops | bytes accessed | tf_op | source)
XLA Modules:
  0.0 190.4 jit_solution(117995942509143312)
XLA Ops:
  0.6 1.0 bitcast_convert_fusion
  1.6 0.0 copy-start.3
  1.6 1.5 bitcast_convert_fusion.1
  3.1 3.0 %collective-permute-start = (bf16[1,16,2816]{2,1,0:T(8,128)(2,1)S(1)}, bf16[1,16,2816]{2,1,0:T(8,128)(2,1)S(1)}, u32[]{:S(2)}, u32[]{:S(2)}) collective-permute-start(bf16[1,16,2816]{2,1,0:T(8,128)(2,1)S(1)} %pad_maximum_fusion.1), channel_id=1, source_target_pairs={{0,16},{16,0},{1,17},{17,1},{2,18},{18,2},{3,19},{19,3},{4,20},{20... | collective-permute-start | bytes 270344 | tf_op jit(solution)/shard_map/ppermute | solution.py:26
  6.1 0.7 bitcast_convert_fusion.2
  6.8 0.7 convert_bitcast_fusion.2
  7.5 0.7 copy.25.cap_ref
  8.2 1.9 pad_maximum_fusion.x_ref
  10.1 1.3 select_reduce_fusion.table_ref
  11.4 0.0 copy-done.3
  11.4 0.0 copy-start.6
  11.4 0.0 copy-start.4
  11.4 0.0 copy-start.2
  11.4 170.0 %shard_map.198 = (bf16[128,2048]{1,0:T(8,128)(2,1)}, f32[16,768]{1,0:T(8,128)}, f32[16,2048]{1,0:T(8,128)}) custom-call(bf16[144,2048]{1,0:T(8,128)(2,1)} %pad_maximum_fusion.x_ref, bf16[128,2048]{1,0:T(8,128)(2,1)} %bitcast.86, f32[16,128]{1,0:T(8,128)} %select_reduce_fusion.table_ref, f32[16,1]{1,0:T(8,128)} %copy.25.cap_ref, bf16[2048,768]{1,0:T(8,128)(2,1)} %bitcast.83, ...), custom_call_target="tpu_custom_call" | custom-call | flops 20000000000 | bytes 30000000 | tf_op jit(solution)/shard_map/pallas_call | solution.py:418
  181.4 0.0 copy-done
  181.5 0.0 copy-done.1
  181.5 1.6 fusion.9
  183.1 0.0 copy-done.5
  183.1 1.4 fusion.11
  185.3 0.0 collective-permute-done
  185.3 1.5 fusion.7
  186.8 0.0 copy-done.2
  186.8 1.7 fusion.3
  188.5 1.9 copy.28
  (7 shorter events, 0.0 us)
Async XLA Ops:
  1.6 9.8 %copy-start.3 = (bf16[16,2048]{1,0:T(8,128)(2,1)}, bf16[16,2048]{1,0:T(8,128)(2,1)S(1)}, u32[]{:S(2)}) copy-start(bf16[16,2048]{1,0:T(8,128)(2,1)S(1)} %get-tuple-element.16.out_ref) | copy-start | bytes 196612
  3.1 182.2 %collective-permute-start = (bf16[1,16,2816]{2,1,0:T(8,128)(2,1)S(1)}, bf16[1,16,2816]{2,1,0:T(8,128)(2,1)S(1)}, u32[]{:S(2)}, u32[]{:S(2)}) collective-permute-start(bf16[1,16,2816]{2,1,0:T(8,128)(2,1)S(1)} %pad_maximum_fusion.1), channel_id=1, source_target_pairs={{0,16},{16,0},{1,17},{17,1},{2,18},{18,2},{3,19},{19,3},{4,20},{20... | collective-permute-start | bytes 270344 | tf_op jit(solution)/shard_map/ppermute | solution.py:26
  11.4 170.1 %copy-start = (f32[1,1,16,2048]{3,2,1,0:T(8,128)S(1)}, f32[1,1,16,2048]{3,2,1,0:T(8,128)}, u32[]{:S(2)}) copy-start(f32[1,1,16,2048]{3,2,1,0:T(8,128)} %param.27) | copy-start | bytes 393220
  11.4 170.1 %copy-start.1 = (f32[1,1,16,2048]{3,2,1,0:T(8,128)S(1)}, f32[1,1,16,2048]{3,2,1,0:T(8,128)}, u32[]{:S(2)}) copy-start(f32[1,1,16,2048]{3,2,1,0:T(8,128)} %param.29) | copy-start | bytes 393220
  11.4 171.7 %copy-start.5 = (f32[1,1,16,768]{3,2,1,0:T(8,128)S(1)}, f32[1,1,16,768]{3,2,1,0:T(8,128)}, u32[]{:S(2)}) copy-start(f32[1,1,16,768]{3,2,1,0:T(8,128)} %param.26) | copy-start | bytes 147460
  11.4 171.7 %copy-start.6 = (f32[1,1,16,768]{3,2,1,0:T(8,128)S(1)}, f32[1,1,16,768]{3,2,1,0:T(8,128)}, u32[]{:S(2)}) copy-start(f32[1,1,16,768]{3,2,1,0:T(8,128)} %param.28) | copy-start | bytes 147460
  11.4 173.9 %copy-start.4 = (f32[1,1,16,768]{3,2,1,0:T(8,128)S(1)}, f32[1,1,16,768]{3,2,1,0:T(8,128)}, u32[]{:S(2)}) copy-start(f32[1,1,16,768]{3,2,1,0:T(8,128)} %param.24) | copy-start | bytes 147460
  11.4 175.4 %copy-start.2 = (f32[1,1,16,2048]{3,2,1,0:T(8,128)S(1)}, f32[1,1,16,2048]{3,2,1,0:T(8,128)}, u32[]{:S(2)}) copy-start(f32[1,1,16,2048]{3,2,1,0:T(8,128)} %param.25) | copy-start | bytes 393220

commit v2 on v1

--- a/solution.py
+++ b/solution.py
@@ -156,7 +156,8 @@
             part.at[zt * 4 + y * 2 + c], from_high.at[zt], z_s.at[zt], zd_r.at[zt], me - 4
         )
 
-    rows[me] = x_ref[...]
+    rows[me, 0:tok, :] = x_ref[...]
+    rows[me, tok : tok + rank, :] = out_ref[...]
     tables[me] = table_ref[...]
     barrier = pltpu.get_barrier_semaphore()
 
@@ -305,6 +306,24 @@
         def _():
             add_core(now, y)
 
+    @pl.loop(0, n)
+    def _(t):
+        @pl.when(t != me)
+        def _():
+            copy(low_mine.at[t], low_got.at[t], low_s.at[t], low_r.at[t], t).wait_recv()
+
+        weighted = (low_got[t].astype(f32) * own_table[pl.ds(t, 1), :]).astype(bf16)
+        grad = adapter_scale * jnp.dot(weighted, cot_ref[...], preferred_element_type=f32)
+
+        @pl.when(t == me)
+        def _():
+            grad_got[t] = grad.astype(bf16)
+
+        @pl.when(t != me)
+        def _():
+            grad_mine[t] = grad.astype(bf16)
+            send_grad(t).start()
+
     @pl.when((z > 0) & (z < depth - 1))
     def _():
         @pl.loop(0, depth - 1)
@@ -324,24 +343,6 @@
                 send_down(zt).wait_recv()
                 part[t] = (part[t].astype(f32) + from_high[zt].astype(f32)).astype(bf16)
                 send_down(zt).start()
-
-    @pl.loop(0, n)
-    def _(t):
-        @pl.when(t != me)
-        def _():
-            copy(low_mine.at[t], low_got.at[t], low_s.at[t], low_r.at[t], t).wait_recv()
-
-        weighted = (low_got[t].astype(f32) * own_table[pl.ds(t, 1), :]).astype(bf16)
-        grad = adapter_scale * jnp.dot(weighted, cot_ref[...], preferred_element_type=f32)
-
-        @pl.when(t == me)
-        def _():
-            grad_got[t] = grad.astype(bf16)
-
-        @pl.when(t != me)
-        def _():
-            grad_mine[t] = grad.astype(bf16)
-            send_grad(t).start()
 
     gin_ref[...] = jnp.zeros_like(gin_ref)
 
@@ -487,7 +488,7 @@
         jnp.where(hits, router_pair_weight[0].astype(jnp.float32)[None], 0.0), axis=2
     )
     combined, grad_in, grad_out = layer(
-        jnp.concatenate((tokens[0], out_b), axis=0),
+        tokens[0],
         own_grads,
         table,
         capacity.astype(jnp.float32)[:, None],

time: 192 us -> 192 us (level)
  Pallas kernels: 170 us -> 173 us
    pallas_call x1, Pallas kernels: 170 us -> 173 us  [layer(): pl.pallas_call(layer_kernel, out_shape=(jax.ShapeDtypeStruct((tok, width)...]
  transfers between devices with their start and end apart: 1 -> 1, of which waited for: 0 -> 0; matrix products, arithmetic and copies ran while one was open for 4% -> 3% of each run, Pallas kernels for 89% -> 90%
where the time goes in v2:
time: 192 us
  Pallas kernels  173 us (90%)
  other arithmetic  12 us (6%)
  starting transfers between devices  3 us (2%)
  local copies, waits for them, and re-layouts  2.59 us (1%)
    pallas_call x1, Pallas kernels, layer(): pl.pallas_call(layer_kernel, out_shape=(jax.ShapeDtypeStruct((tok, width)...  173 us
  transfers between devices with their start and end apart: 1, of which 0 were waited for; matrix products, arithmetic and copies ran while one was open for 3% of the time, Pallas kernels for 90%

profile of v2, /device:TPU:0, one launch (start us, length us, event | category | flops | bytes accessed | tf_op | source)
XLA Modules:
  0.0 192.0 jit_solution(10427797022726381663)
XLA Ops:
  0.6 1.5 bitcast_convert_fusion.1
  2.1 1.6 bitcast_convert_fusion
  3.8 3.0 %collective-permute-start = (bf16[1,16,2816]{2,1,0:T(8,128)(2,1)S(1)}, bf16[1,16,2816]{2,1,0:T(8,128)(2,1)S(1)}, u32[]{:S(2)}, u32[]{:S(2)}) collective-permute-start(bf16[1,16,2816]{2,1,0:T(8,128)(2,1)S(1)} %pad_maximum_fusion), channel_id=1, source_target_pairs={{0,16},{16,0},{1,17},{17,1},{2,18},{18,2},{3,19},{19,3},{4,20},{20... | collective-permute-start | bytes 270344 | tf_op jit(solution)/shard_map/ppermute | solution.py:26
  6.8 0.7 bitcast_convert_fusion.2
  7.4 0.7 convert_bitcast_fusion.2
  8.1 0.7 copy.25.cap_ref
  8.8 1.3 select_reduce_fusion.table_ref
  10.1 0.0 copy-start
  10.1 0.0 copy-start.1
  10.1 0.0 copy-start.4
  10.1 0.0 copy-start.2
  10.1 173.0 %shard_map.198 = (bf16[128,2048]{1,0:T(8,128)(2,1)}, f32[16,768]{1,0:T(8,128)}, f32[16,2048]{1,0:T(8,128)}) custom-call(bf16[128,2048]{1,0:T(8,128)(2,1)} %bitcast.85, bf16[128,2048]{1,0:T(8,128)(2,1)} %bitcast.86, f32[16,128]{1,0:T(8,128)} %select_reduce_fusion.table_ref, f32[16,1]{1,0:T(8,128)} %copy.25.cap_ref, bf16[2048,768]{1,0:T(8,128)(2,1)} %bitcast.82, ...), custom_call_target="tpu_custom_call" | custom-call | flops 20000000000 | bytes 30000000 | tf_op jit(solution)/shard_map/pallas_call | solution.py:419
  183.1 0.0 copy-done
  183.1 0.0 copy-done.1
  183.1 1.6 fusion.9
  184.7 0.0 copy-done.4
  184.8 0.0 copy-done.5
  184.8 1.4 fusion.11
  186.9 0.0 collective-permute-done
  187.0 0.0 copy-done.3
  187.0 1.5 fusion.7
  188.5 0.0 copy-done.2
  188.5 1.7 fusion.3
  190.1 1.9 copy.28
  (4 shorter events, 0.0 us)
Async XLA Ops:
  3.8 183.2 %collective-permute-start = (bf16[1,16,2816]{2,1,0:T(8,128)(2,1)S(1)}, bf16[1,16,2816]{2,1,0:T(8,128)(2,1)S(1)}, u32[]{:S(2)}, u32[]{:S(2)}) collective-permute-start(bf16[1,16,2816]{2,1,0:T(8,128)(2,1)S(1)} %pad_maximum_fusion), channel_id=1, source_target_pairs={{0,16},{16,0},{1,17},{17,1},{2,18},{18,2},{3,19},{19,3},{4,20},{20... | collective-permute-start | bytes 270344 | tf_op jit(solution)/shard_map/ppermute | solution.py:26
  10.1 173.0 %copy-start = (f32[1,1,16,2048]{3,2,1,0:T(8,128)S(1)}, f32[1,1,16,2048]{3,2,1,0:T(8,128)}, u32[]{:S(2)}) copy-start(f32[1,1,16,2048]{3,2,1,0:T(8,128)} %param.27) | copy-start | bytes 393220
  10.1 173.0 %copy-start.1 = (f32[1,1,16,2048]{3,2,1,0:T(8,128)S(1)}, f32[1,1,16,2048]{3,2,1,0:T(8,128)}, u32[]{:S(2)}) copy-start(f32[1,1,16,2048]{3,2,1,0:T(8,128)} %param.29) | copy-start | bytes 393220
  10.1 174.7 %copy-start.4 = (f32[1,1,16,768]{3,2,1,0:T(8,128)S(1)}, f32[1,1,16,768]{3,2,1,0:T(8,128)}, u32[]{:S(2)}) copy-start(f32[1,1,16,768]{3,2,1,0:T(8,128)} %param.26) | copy-start | bytes 147460
  10.1 174.7 %copy-start.5 = (f32[1,1,16,768]{3,2,1,0:T(8,128)S(1)}, f32[1,1,16,768]{3,2,1,0:T(8,128)}, u32[]{:S(2)}) copy-start(f32[1,1,16,768]{3,2,1,0:T(8,128)} %param.28) | copy-start | bytes 147460
  10.1 176.9 %copy-start.3 = (f32[1,1,16,768]{3,2,1,0:T(8,128)S(1)}, f32[1,1,16,768]{3,2,1,0:T(8,128)}, u32[]{:S(2)}) copy-start(f32[1,1,16,768]{3,2,1,0:T(8,128)} %param.24) | copy-start | bytes 147460
  10.1 178.4 %copy-start.2 = (f32[1,1,16,2048]{3,2,1,0:T(8,128)S(1)}, f32[1,1,16,2048]{3,2,1,0:T(8,128)}, u32[]{:S(2)}) copy-start(f32[1,1,16,2048]{3,2,1,0:T(8,128)} %param.25) | copy-start | bytes 393220

commit v3 on v1

--- a/solution.py
+++ b/solution.py
@@ -156,7 +156,8 @@
             part.at[zt * 4 + y * 2 + c], from_high.at[zt], z_s.at[zt], zd_r.at[zt], me - 4
         )
 
-    rows[me] = x_ref[...]
+    rows[me, 0:tok, :] = x_ref[...]
+    rows[me, tok : tok + rank, :] = out_ref[...]
     tables[me] = table_ref[...]
     barrier = pltpu.get_barrier_semaphore()
 
@@ -282,6 +283,11 @@
                 wait_rows(zt * 4 + yt * 2 + 1 - c)
                 expert_pair(zt, yt)
 
+        @pl.when((s > 0) & (s <= depth))
+        def _():
+            add_core(last, 1 - y)
+            send_y(last).start()
+
         @pl.when(s >= 2)
         def _():
             t = older * 4 + y * 2 + c
@@ -295,11 +301,6 @@
             @pl.when((z == depth - 1) & (older < depth - 1))
             def _():
                 send_down(older).start()
-
-        @pl.when((s > 0) & (s <= depth))
-        def _():
-            add_core(last, 1 - y)
-            send_y(last).start()
 
         @pl.when(s < depth)
         def _():
@@ -326,7 +327,9 @@
                 send_down(zt).start()
 
     @pl.loop(0, n)
-    def _(t):
+    def _(d):
+        t = lax.rem(me + d, n)
+
         @pl.when(t != me)
         def _():
             copy(low_mine.at[t], low_got.at[t], low_s.at[t], low_r.at[t], t).wait_recv()
@@ -487,7 +490,7 @@
         jnp.where(hits, router_pair_weight[0].astype(jnp.float32)[None], 0.0), axis=2
     )
     combined, grad_in, grad_out = layer(
-        jnp.concatenate((tokens[0], out_b), axis=0),
+        tokens[0],
         own_grads,
         table,
         capacity.astype(jnp.float32)[:, None],

time: 192 us -> 191 us (level)
  transfers between devices with their start and end apart: 1 -> 1, of which waited for: 0 -> 0; matrix products, arithmetic and copies ran while one was open for 4% -> 3% of each run, Pallas kernels for 89% -> 90%
where the time goes in v3:
time: 191 us; the launch traced here: 189 us
  Pallas kernels  170 us (89%)
  other arithmetic  12 us (6%)
  starting transfers between devices  3 us (2%)
  local copies, waits for them, and re-layouts  2.59 us (1%)
    pallas_call x1, Pallas kernels, layer(): pl.pallas_call(layer_kernel, out_shape=(jax.ShapeDtypeStruct((tok, width)...  170 us
  transfers between devices with their start and end apart: 1, of which 0 were waited for; matrix products, arithmetic and copies ran while one was open for 3% of the time, Pallas kernels for 90%

profile of v3, /device:TPU:0, one launch (start us, length us, event | category | flops | bytes accessed | tf_op | source)
XLA Modules:
  0.0 189.2 jit_solution(13439475481429199271)
XLA Ops:
  0.6 1.5 bitcast_convert_fusion.1
  2.1 1.6 bitcast_convert_fusion
  3.8 3.0 %collective-permute-start = (bf16[1,16,2816]{2,1,0:T(8,128)(2,1)S(1)}, bf16[1,16,2816]{2,1,0:T(8,128)(2,1)S(1)}, u32[]{:S(2)}, u32[]{:S(2)}) collective-permute-start(bf16[1,16,2816]{2,1,0:T(8,128)(2,1)S(1)} %pad_maximum_fusion), channel_id=1, source_target_pairs={{0,16},{16,0},{1,17},{17,1},{2,18},{18,2},{3,19},{19,3},{4,20},{20... | collective-permute-start | bytes 270344 | tf_op jit(solution)/shard_map/ppermute | solution.py:26
  6.8 0.7 bitcast_convert_fusion.2
  7.4 0.7 convert_bitcast_fusion.2
  8.1 0.7 copy.25.cap_ref
  8.8 1.3 select_reduce_fusion.table_ref
  10.1 0.0 copy-start
  10.1 0.0 copy-start.1
  10.1 0.0 copy-start.4
  10.1 0.0 copy-start.2
  10.1 170.1 %shard_map.198 = (bf16[128,2048]{1,0:T(8,128)(2,1)}, f32[16,768]{1,0:T(8,128)}, f32[16,2048]{1,0:T(8,128)}) custom-call(bf16[128,2048]{1,0:T(8,128)(2,1)} %bitcast.85, bf16[128,2048]{1,0:T(8,128)(2,1)} %bitcast.86, f32[16,128]{1,0:T(8,128)} %select_reduce_fusion.table_ref, f32[16,1]{1,0:T(8,128)} %copy.25.cap_ref, bf16[2048,768]{1,0:T(8,128)(2,1)} %bitcast.82, ...), custom_call_target="tpu_custom_call" | custom-call | flops 20000000000 | bytes 30000000 | tf_op jit(solution)/shard_map/pallas_call | solution.py:421
  180.3 0.0 copy-done
  180.3 0.0 copy-done.1
  180.3 1.6 fusion.9
  181.9 0.0 copy-done.4
  181.9 0.0 copy-done.5
  181.9 1.4 fusion.11
  184.1 0.0 collective-permute-done
  184.1 0.0 copy-done.3
  184.2 1.5 fusion.7
  185.6 0.0 copy-done.2
  185.6 1.7 fusion.3
  187.3 1.9 copy.28
  (4 shorter events, 0.0 us)
Async XLA Ops:
  3.8 180.4 %collective-permute-start = (bf16[1,16,2816]{2,1,0:T(8,128)(2,1)S(1)}, bf16[1,16,2816]{2,1,0:T(8,128)(2,1)S(1)}, u32[]{:S(2)}, u32[]{:S(2)}) collective-permute-start(bf16[1,16,2816]{2,1,0:T(8,128)(2,1)S(1)} %pad_maximum_fusion), channel_id=1, source_target_pairs={{0,16},{16,0},{1,17},{17,1},{2,18},{18,2},{3,19},{19,3},{4,20},{20... | collective-permute-start | bytes 270344 | tf_op jit(solution)/shard_map/ppermute | solution.py:26
  10.1 170.2 %copy-start = (f32[1,1,16,2048]{3,2,1,0:T(8,128)S(1)}, f32[1,1,16,2048]{3,2,1,0:T(8,128)}, u32[]{:S(2)}) copy-start(f32[1,1,16,2048]{3,2,1,0:T(8,128)} %param.27) | copy-start | bytes 393220
  10.1 170.2 %copy-start.1 = (f32[1,1,16,2048]{3,2,1,0:T(8,128)S(1)}, f32[1,1,16,2048]{3,2,1,0:T(8,128)}, u32[]{:S(2)}) copy-start(f32[1,1,16,2048]{3,2,1,0:T(8,128)} %param.29) | copy-start | bytes 393220
  10.1 171.8 %copy-start.4 = (f32[1,1,16,768]{3,2,1,0:T(8,128)S(1)}, f32[1,1,16,768]{3,2,1,0:T(8,128)}, u32[]{:S(2)}) copy-start(f32[1,1,16,768]{3,2,1,0:T(8,128)} %param.26) | copy-start | bytes 147460
  10.1 171.8 %copy-start.5 = (f32[1,1,16,768]{3,2,1,0:T(8,128)S(1)}, f32[1,1,16,768]{3,2,1,0:T(8,128)}, u32[]{:S(2)}) copy-start(f32[1,1,16,768]{3,2,1,0:T(8,128)} %param.28) | copy-start | bytes 147460
  10.1 174.0 %copy-start.3 = (f32[1,1,16,768]{3,2,1,0:T(8,128)S(1)}, f32[1,1,16,768]{3,2,1,0:T(8,128)}, u32[]{:S(2)}) copy-start(f32[1,1,16,768]{3,2,1,0:T(8,128)} %param.24) | copy-start | bytes 147460
  10.1 175.5 %copy-start.2 = (f32[1,1,16,2048]{3,2,1,0:T(8,128)S(1)}, f32[1,1,16,2048]{3,2,1,0:T(8,128)}, u32[]{:S(2)}) copy-start(f32[1,1,16,2048]{3,2,1,0:T(8,128)} %param.25) | copy-start | bytes 393220
